TPU v7x, 128 devices: a whole 4x4x4 slice. The times are simulated.
128 devices in a mesh: ctx: 32 (over z, x, y_lo), tp: 4 (over y_hi, core).
Axes of the slice: x: 4, y: 4 (y_hi: 2, y_lo: 2; y = y_hi * 2 + y_lo), z: 4, core: 2. Of those that a mesh axis runs over, the one named last changes fastest.
Arguments:
- signal: bfloat16 [4096, 2048], P('ctx', 'tp'), may hold values from -6 to 6
- gate: bfloat16 [4096, 2048], P('ctx', 'tp'), may hold values from -6 to 6
- filt: bfloat16 [4096, 2048], P('ctx', 'tp'), may hold values from -0.25 to 0.25
- bias: float32 [2048], P('tp'), may hold values from -2 to 2
- doc_ids: int32 [4096], replicated, may hold values from 0 to 3, never falling along the last dimension, each value on 1 to 3840 neighbouring positions
- block_perm: int32 [64], replicated, may hold values from 0 to 63, each once
- out_weight: bfloat16 [2048, 2048], P('tp'), may hold values from -0.125 to 0.125
Outputs:
- mixed: bfloat16 [4096, 2048], P('ctx', 'tp')
Inputs may be any that keep to these rules, and one draw needn't show every extreme that they name: `doc_ids`: ids never fall along the sequence; each document is a run of 1 to 3840 positions, one exactly 3840. `block_perm`: each block number once.
All inputs are finite; a program needn't handle non-finite values.
Results may differ from a plain program's by a relative error of at most 0.012.
Values may be sent and summed in bfloat16 or wider, within the bound.
No kernel may reach another device: no remote copies, remote signals or barrier semaphores. Data moves between devices by JAX's collectives and lax.ppermute only.
A program may use at most 64 MiB of HBM per device.

v0:
```python
import math
import jax
import jax.numpy as jnp
from jax import lax
from jax.sharding import PartitionSpec as P

SPAN = 64


def split_table(table):
    upper_part = table.astype(jnp.bfloat16)
    lower_part = (table - upper_part.astype(jnp.float32)).astype(jnp.bfloat16)
    return (upper_part, lower_part)


def transform_many(divide_pair_table, input_values):
    first_position = jnp.einsum(
        "ol,wld->wod", divide_pair_table[0], input_values, preferred_element_type=jnp.float32
    )
    return first_position + jnp.einsum(
        "ol,wld->wod", divide_pair_table[1], input_values, preferred_element_type=jnp.float32
    )


def group_size():
    return 4


def body(signal, gate, filt, bias, doc_ids, block_perm, out_weight):
    block_len = SPAN
    frame_len = 2 * block_len
    channels = signal.shape[1]
    highest_index = lax.Precision.HIGHEST
    whole_filter = lax.all_gather(filt, "ctx", axis=0, tiled=True)
    positions = jnp.arange(frame_len, dtype=jnp.int32)
    phase_idx = positions[:, None] * positions[None, :] % frame_len
    angles = phase_idx.astype(jnp.float32) * (2.0 * math.pi / frame_len)
    cos_tab = jnp.cos(angles)
    sin_tab = jnp.sin(angles)
    cos_kernel = split_table(cos_tab[:, : frame_len - 1])
    sin_kernel = split_table(sin_tab[:, : frame_len - 1])
    cos_source = split_table(cos_tab[:, :block_len])
    sine_source_rows = split_table(sin_tab[:, :block_len])
    cycle_pos = lax.axis_index("ctx")
    own_blocks = lax.dynamic_slice_in_dim(block_perm, 2 * cycle_pos, 2)
    target_blocks = [own_blocks[0], own_blocks[1]]
    target_docs = [
        lax.dynamic_slice_in_dim(doc_ids, number * block_len, block_len) for number in target_blocks
    ]
    lead_docs = [docs[0] for docs in target_docs]
    own_rows = [signal[:block_len], signal[block_len:]]

    def block_docs(number):
        return lax.dynamic_slice_in_dim(doc_ids, number * block_len, block_len)

    def filter_window(lag_blocks):
        return lax.dynamic_slice_in_dim(
            whole_filter, lag_blocks * block_len - block_len + 1, frame_len - 1, 0
        )

    def pair_spectra(sources, source_numbers, target_numbers, leads):
        source_docs = jax.vmap(block_docs)(source_numbers)
        keep_rows = (source_docs == leads[:, None]) & (source_numbers < target_numbers)[:, None]
        masked = jnp.where(keep_rows[:, :, None], sources, jnp.zeros_like(sources))
        lag_blocks = jnp.maximum(target_numbers - source_numbers, 1)
        windows = jax.vmap(filter_window)(lag_blocks)
        kernel_re = transform_many(cos_kernel, windows)
        kernel_im = -transform_many(sin_kernel, windows)
        source_re = transform_many(cos_source, masked)
        source_im = -transform_many(sine_source_rows, masked)
        return (
            kernel_re * source_re - kernel_im * source_im,
            kernel_re * source_im + kernel_im * source_re,
        )

    def inverse(spec_re, spec_im, docs, lead_doc):
        values = jnp.dot(cos_tab[block_len - 1 : frame_len - 1], spec_re, precision=highest_index)
        values = values - jnp.dot(
            sin_tab[block_len - 1 : frame_len - 1], spec_im, precision=highest_index
        )
        return jnp.where((docs == lead_doc)[:, None], values / frame_len, 0.0)

    zero_spec = jnp.zeros((frame_len, channels), jnp.float32)
    totals = (zero_spec, zero_spec, zero_spec, zero_spec)
    arrived = lax.all_gather(signal, "ctx", axis=0, tiled=True)
    block_count = arrived.shape[0] // block_len
    group = group_size()
    steps = block_count // group
    arrived_groups = arrived.reshape(steps, group, block_len, channels)

    def absorb_group(running, item):
        group_rows, step_index = item
        numbers = lax.dynamic_slice_in_dim(block_perm, step_index * group, group)
        sources = jnp.concatenate([group_rows, group_rows], axis=0)
        source_numbers = jnp.concatenate([numbers, numbers], axis=0)
        target_numbers = jnp.concatenate(
            [
                jnp.full((group,), target_blocks[0], jnp.int32),
                jnp.full((group,), target_blocks[1], jnp.int32),
            ],
            axis=0,
        )
        leads = jnp.concatenate(
            [
                jnp.full((group,), lead_docs[0], jnp.int32),
                jnp.full((group,), lead_docs[1], jnp.int32),
            ],
            axis=0,
        )
        part_re, part_im = pair_spectra(sources, source_numbers, target_numbers, leads)
        part_re = part_re.reshape(2, group, frame_len, channels).sum(axis=1)
        part_im = part_im.reshape(2, group, frame_len, channels).sum(axis=1)
        return (
            (
                running[0] + part_re[0],
                running[1] + part_im[0],
                running[2] + part_re[1],
                running[3] + part_im[1],
            ),
            None,
        )

    totals, unused = lax.scan(
        absorb_group, totals, (arrived_groups, jnp.arange(steps, dtype=jnp.int32))
    )
    distant = [
        inverse(totals[2 * slot], totals[2 * slot + 1], target_docs[slot], lead_docs[slot])
        for slot in range(2)
    ]
    offsets = positions[:block_len][:, None] - positions[:block_len][None, :]
    near_taps = whole_filter[:block_len]
    gathered_taps = near_taps[jnp.maximum(offsets, 0)]
    gated_parts = []
    for slot in range(2):
        docs = target_docs[slot]
        allowed = (offsets >= 0) & (docs[:, None] == docs[None, :])
        toeplitz = jnp.where(allowed[:, :, None], gathered_taps, jnp.zeros_like(gathered_taps))
        local_part = jnp.einsum(
            "tsc,sc->tc", toeplitz, own_rows[slot], preferred_element_type=jnp.float32
        )
        source = own_rows[slot].astype(jnp.float32)
        gate_rows = gate[slot * block_len : (slot + 1) * block_len].astype(jnp.float32)
        gated_parts.append(
            (gate_rows * (local_part + distant[slot] + bias[None, :] * source)).astype(jnp.bfloat16)
        )
    gated = jnp.concatenate(gated_parts, axis=0)
    partial_value = jnp.dot(gated, out_weight, preferred_element_type=jnp.float32)
    return lax.psum_scatter(partial_value, "tp", scatter_dimension=1, tiled=True).astype(
        jnp.bfloat16
    )


def solution(mesh):
    return jax.shard_map(
        body,
        mesh=mesh,
        in_specs=(P("ctx", "tp"), P("ctx", "tp"), P("ctx", "tp"), P("tp"), P(), P(), P("tp", None)),
        out_specs=P("ctx", "tp"),
        check_vma=False,
    )
```

profile of v0, /device:TPU:1, one launch (start us, length us, event | category | flops | bytes accessed | tf_op | source)
XLA Modules:
  0.0 1316.1 jit_solution(3132769725770774739)
XLA Ops:
  22.6 127.1 %all-gather.3.cloned.1.call-done = bf16[4096,512]{1,0:T(8,128)(2,1)} async-done(((bf16[128,512]{1,0:T(8,128)(2,1)}), bf16[4096,512]{1,0:T(8,128)(2,1)}) %all-gather.3.cloned.1.call-update) | async-done | bytes 4194320 | tf_op jit(solution)/shard_map/all_gather | solution.py:34
  149.7 158.3 %all-gather.5.cloned.1.call-done = bf16[4096,512]{1,0:T(8,128)(2,1)} async-done(((bf16[128,512]{1,0:T(8,128)(2,1)}), bf16[4096,512]{1,0:T(8,128)(2,1)}) %all-gather.5.cloned.1.call-update) | async-done | bytes 4194320 | tf_op jit(solution)/shard_map/all_gather | solution.py:85
  308.5 916.3 %while.29 = (s32[]{:T(128)}, f32[128,512]{0,1:T(8,128)}, f32[128,512]{0,1:T(8,128)}, f32[128,512]{0,1:T(8,128)}, f32[128,512]{0,1:T(8,128)}, /*index=5*/s32[]{:T...) while((s32[]{:T(128)}, f32[128,512]{0,1:T(8,128)}, ...), condition=%wide.region_3.4_spmd.clone, body=%wide.region_0.3_spmd.clone.sunk | while | flops 810812544 | bytes 56596156 | solution.py:123
  312.6 17.9 %while.30 = (s32[]{:T(128)}, bf16[4096,512]{1,0:T(8,128)(2,1)}, s32[8,2]{0,1:T(2,128)S(1)}, bf16[8,127,512]{2,1,0:T(8,128)(2,1)S(1)}, s32[]{:T(128)}) while((s32[]{:T(128)}, bf16[4096,512]{1,0:T(8,128)(2,1)}, s32[8,2]{0,1:T(2,128)S(1)}, bf16[8,127,512]{2,1,0:T(8,128)(2,1)S(1)}, s32[]{:T(128)}) %tuple.94), condition=%wide.while_cond, body=%wide.while_body.sunk | while | flops 2 | bytes 261225 | solution.py:57
  368.8 17.9 %while.30 = (s32[]{:T(128)}, bf16[4096,512]{1,0:T(8,128)(2,1)}, s32[8,2]{0,1:T(2,128)S(1)}, bf16[8,127,512]{2,1,0:T(8,128)(2,1)S(1)}, s32[]{:T(128)}) while((s32[]{:T(128)}, bf16[4096,512]{1,0:T(8,128)(2,1)}, s32[8,2]{0,1:T(2,128)S(1)}, bf16[8,127,512]{2,1,0:T(8,128)(2,1)S(1)}, s32[]{:T(128)}) %tuple.94), condition=%wide.while_cond, body=%wide.while_body.sunk | while | flops 2 | bytes 261225 | solution.py:57
  426.2 17.9 %while.30 = (s32[]{:T(128)}, bf16[4096,512]{1,0:T(8,128)(2,1)}, s32[8,2]{0,1:T(2,128)S(1)}, bf16[8,127,512]{2,1,0:T(8,128)(2,1)S(1)}, s32[]{:T(128)}) while((s32[]{:T(128)}, bf16[4096,512]{1,0:T(8,128)(2,1)}, s32[8,2]{0,1:T(2,128)S(1)}, bf16[8,127,512]{2,1,0:T(8,128)(2,1)S(1)}, s32[]{:T(128)}) %tuple.94), condition=%wide.while_cond, body=%wide.while_body.sunk | while | flops 2 | bytes 261225 | solution.py:57
  483.5 17.9 %while.30 = (s32[]{:T(128)}, bf16[4096,512]{1,0:T(8,128)(2,1)}, s32[8,2]{0,1:T(2,128)S(1)}, bf16[8,127,512]{2,1,0:T(8,128)(2,1)S(1)}, s32[]{:T(128)}) while((s32[]{:T(128)}, bf16[4096,512]{1,0:T(8,128)(2,1)}, s32[8,2]{0,1:T(2,128)S(1)}, bf16[8,127,512]{2,1,0:T(8,128)(2,1)S(1)}, s32[]{:T(128)}) %tuple.94), condition=%wide.while_cond, body=%wide.while_body.sunk | while | flops 2 | bytes 261225 | solution.py:57
  540.8 17.9 %while.30 = (s32[]{:T(128)}, bf16[4096,512]{1,0:T(8,128)(2,1)}, s32[8,2]{0,1:T(2,128)S(1)}, bf16[8,127,512]{2,1,0:T(8,128)(2,1)S(1)}, s32[]{:T(128)}) while((s32[]{:T(128)}, bf16[4096,512]{1,0:T(8,128)(2,1)}, s32[8,2]{0,1:T(2,128)S(1)}, bf16[8,127,512]{2,1,0:T(8,128)(2,1)S(1)}, s32[]{:T(128)}) %tuple.94), condition=%wide.while_cond, body=%wide.while_body.sunk | while | flops 2 | bytes 261225 | solution.py:57
  598.2 17.9 %while.30 = (s32[]{:T(128)}, bf16[4096,512]{1,0:T(8,128)(2,1)}, s32[8,2]{0,1:T(2,128)S(1)}, bf16[8,127,512]{2,1,0:T(8,128)(2,1)S(1)}, s32[]{:T(128)}) while((s32[]{:T(128)}, bf16[4096,512]{1,0:T(8,128)(2,1)}, s32[8,2]{0,1:T(2,128)S(1)}, bf16[8,127,512]{2,1,0:T(8,128)(2,1)S(1)}, s32[]{:T(128)}) %tuple.94), condition=%wide.while_cond, body=%wide.while_body.sunk | while | flops 2 | bytes 261225 | solution.py:57
  655.5 17.9 %while.30 = (s32[]{:T(128)}, bf16[4096,512]{1,0:T(8,128)(2,1)}, s32[8,2]{0,1:T(2,128)S(1)}, bf16[8,127,512]{2,1,0:T(8,128)(2,1)S(1)}, s32[]{:T(128)}) while((s32[]{:T(128)}, bf16[4096,512]{1,0:T(8,128)(2,1)}, s32[8,2]{0,1:T(2,128)S(1)}, bf16[8,127,512]{2,1,0:T(8,128)(2,1)S(1)}, s32[]{:T(128)}) %tuple.94), condition=%wide.while_cond, body=%wide.while_body.sunk | while | flops 2 | bytes 261225 | solution.py:57
  682.2 17.1 %while.31 = (s32[]{:T(128)}, s32[4096]{0:T(1024)}, s32[8,1]{0,1:T(1,128)S(1)}, s32[8,64]{1,0:T(8,128)S(1)}, s32[]{:T(128)}, /*index=5*/s32[]{:T(128)}) while((s32[]{:T(128)}, s32[4096]{0:T(1024)}, s32[8,1]{0,1:T(1,128)S(1)}, s32[8,64]{1,0:T(8,128)S(1)}, s32[]{:T(128)}, /*index=5*/s32[]{:T(128)}) %tuple.97), condition=%wide.while_cond.1, body=%wide.while_body.1.sunk | while | flops 2 | bytes 1121 | solution.py:54
  712.9 17.9 %while.30 = (s32[]{:T(128)}, bf16[4096,512]{1,0:T(8,128)(2,1)}, s32[8,2]{0,1:T(2,128)S(1)}, bf16[8,127,512]{2,1,0:T(8,128)(2,1)S(1)}, s32[]{:T(128)}) while((s32[]{:T(128)}, bf16[4096,512]{1,0:T(8,128)(2,1)}, s32[8,2]{0,1:T(2,128)S(1)}, bf16[8,127,512]{2,1,0:T(8,128)(2,1)S(1)}, s32[]{:T(128)}) %tuple.94), condition=%wide.while_cond, body=%wide.while_body.sunk | while | flops 2 | bytes 261225 | solution.py:57
  739.6 17.1 %while.31 = (s32[]{:T(128)}, s32[4096]{0:T(1024)}, s32[8,1]{0,1:T(1,128)S(1)}, s32[8,64]{1,0:T(8,128)S(1)}, s32[]{:T(128)}, /*index=5*/s32[]{:T(128)}) while((s32[]{:T(128)}, s32[4096]{0:T(1024)}, s32[8,1]{0,1:T(1,128)S(1)}, s32[8,64]{1,0:T(8,128)S(1)}, s32[]{:T(128)}, /*index=5*/s32[]{:T(128)}) %tuple.97), condition=%wide.while_cond.1, body=%wide.while_body.1.sunk | while | flops 2 | bytes 1121 | solution.py:54
  770.3 17.9 %while.30 = (s32[]{:T(128)}, bf16[4096,512]{1,0:T(8,128)(2,1)}, s32[8,2]{0,1:T(2,128)S(1)}, bf16[8,127,512]{2,1,0:T(8,128)(2,1)S(1)}, s32[]{:T(128)}) while((s32[]{:T(128)}, bf16[4096,512]{1,0:T(8,128)(2,1)}, s32[8,2]{0,1:T(2,128)S(1)}, bf16[8,127,512]{2,1,0:T(8,128)(2,1)S(1)}, s32[]{:T(128)}) %tuple.94), condition=%wide.while_cond, body=%wide.while_body.sunk | while | flops 2 | bytes 261225 | solution.py:57
  827.6 17.9 %while.30 = (s32[]{:T(128)}, bf16[4096,512]{1,0:T(8,128)(2,1)}, s32[8,2]{0,1:T(2,128)S(1)}, bf16[8,127,512]{2,1,0:T(8,128)(2,1)S(1)}, s32[]{:T(128)}) while((s32[]{:T(128)}, bf16[4096,512]{1,0:T(8,128)(2,1)}, s32[8,2]{0,1:T(2,128)S(1)}, bf16[8,127,512]{2,1,0:T(8,128)(2,1)S(1)}, s32[]{:T(128)}) %tuple.94), condition=%wide.while_cond, body=%wide.while_body.sunk | while | flops 2 | bytes 261225 | solution.py:57
  854.3 17.1 %while.31 = (s32[]{:T(128)}, s32[4096]{0:T(1024)}, s32[8,1]{0,1:T(1,128)S(1)}, s32[8,64]{1,0:T(8,128)S(1)}, s32[]{:T(128)}, /*index=5*/s32[]{:T(128)}) while((s32[]{:T(128)}, s32[4096]{0:T(1024)}, s32[8,1]{0,1:T(1,128)S(1)}, s32[8,64]{1,0:T(8,128)S(1)}, s32[]{:T(128)}, /*index=5*/s32[]{:T(128)}) %tuple.97), condition=%wide.while_cond.1, body=%wide.while_body.1.sunk | while | flops 2 | bytes 1121 | solution.py:54
  885.0 17.9 %while.30 = (s32[]{:T(128)}, bf16[4096,512]{1,0:T(8,128)(2,1)}, s32[8,2]{0,1:T(2,128)S(1)}, bf16[8,127,512]{2,1,0:T(8,128)(2,1)S(1)}, s32[]{:T(128)}) while((s32[]{:T(128)}, bf16[4096,512]{1,0:T(8,128)(2,1)}, s32[8,2]{0,1:T(2,128)S(1)}, bf16[8,127,512]{2,1,0:T(8,128)(2,1)S(1)}, s32[]{:T(128)}) %tuple.94), condition=%wide.while_cond, body=%wide.while_body.sunk | while | flops 2 | bytes 261225 | solution.py:57
  942.3 17.9 %while.30 = (s32[]{:T(128)}, bf16[4096,512]{1,0:T(8,128)(2,1)}, s32[8,2]{0,1:T(2,128)S(1)}, bf16[8,127,512]{2,1,0:T(8,128)(2,1)S(1)}, s32[]{:T(128)}) while((s32[]{:T(128)}, bf16[4096,512]{1,0:T(8,128)(2,1)}, s32[8,2]{0,1:T(2,128)S(1)}, bf16[8,127,512]{2,1,0:T(8,128)(2,1)S(1)}, s32[]{:T(128)}) %tuple.94), condition=%wide.while_cond, body=%wide.while_body.sunk | while | flops 2 | bytes 261225 | solution.py:57
  999.6 17.9 %while.30 = (s32[]{:T(128)}, bf16[4096,512]{1,0:T(8,128)(2,1)}, s32[8,2]{0,1:T(2,128)S(1)}, bf16[8,127,512]{2,1,0:T(8,128)(2,1)S(1)}, s32[]{:T(128)}) while((s32[]{:T(128)}, bf16[4096,512]{1,0:T(8,128)(2,1)}, s32[8,2]{0,1:T(2,128)S(1)}, bf16[8,127,512]{2,1,0:T(8,128)(2,1)S(1)}, s32[]{:T(128)}) %tuple.94), condition=%wide.while_cond, body=%wide.while_body.sunk | while | flops 2 | bytes 261225 | solution.py:57
  1057.0 17.9 %while.30 = (s32[]{:T(128)}, bf16[4096,512]{1,0:T(8,128)(2,1)}, s32[8,2]{0,1:T(2,128)S(1)}, bf16[8,127,512]{2,1,0:T(8,128)(2,1)S(1)}, s32[]{:T(128)}) while((s32[]{:T(128)}, bf16[4096,512]{1,0:T(8,128)(2,1)}, s32[8,2]{0,1:T(2,128)S(1)}, bf16[8,127,512]{2,1,0:T(8,128)(2,1)S(1)}, s32[]{:T(128)}) %tuple.94), condition=%wide.while_cond, body=%wide.while_body.sunk | while | flops 2 | bytes 261225 | solution.py:57
  1114.3 17.9 %while.30 = (s32[]{:T(128)}, bf16[4096,512]{1,0:T(8,128)(2,1)}, s32[8,2]{0,1:T(2,128)S(1)}, bf16[8,127,512]{2,1,0:T(8,128)(2,1)S(1)}, s32[]{:T(128)}) while((s32[]{:T(128)}, bf16[4096,512]{1,0:T(8,128)(2,1)}, s32[8,2]{0,1:T(2,128)S(1)}, bf16[8,127,512]{2,1,0:T(8,128)(2,1)S(1)}, s32[]{:T(128)}) %tuple.94), condition=%wide.while_cond, body=%wide.while_body.sunk | while | flops 2 | bytes 261225 | solution.py:57
  1171.7 17.9 %while.30 = (s32[]{:T(128)}, bf16[4096,512]{1,0:T(8,128)(2,1)}, s32[8,2]{0,1:T(2,128)S(1)}, bf16[8,127,512]{2,1,0:T(8,128)(2,1)S(1)}, s32[]{:T(128)}) while((s32[]{:T(128)}, bf16[4096,512]{1,0:T(8,128)(2,1)}, s32[8,2]{0,1:T(2,128)S(1)}, bf16[8,127,512]{2,1,0:T(8,128)(2,1)S(1)}, s32[]{:T(128)}) %tuple.94), condition=%wide.while_cond, body=%wide.while_body.sunk | while | flops 2 | bytes 261225 | solution.py:57
  1228.7 18.7 %gather_fusion = bf16[4096,512]{1,0:T(8,128)(2,1)} fusion(bf16[64,512]{1,0:T(8,128)(2,1)S(1)} %slice.146, s32[4096]{0:T(1024)} %broadcast_clamp_fusion), kind=kCustom, calls=%fused_computation | custom fusion | bytes 8404992 | tf_op jit(solution)/shard_map/gather | solution.py:132
  1256.1 51.8 %reduce-scatter.2.cloned.1.call-done = f32[128,512]{1,0:T(8,128)} async-done(((f32[128,2048]{1,0:T(8,128)}), f32[128,512]{1,0:T(8,128)}) %reduce-scatter.2.cloned.1.call-update) | async-done | bytes 262160 | tf_op jit(solution)/shard_map/reduce_scatter | solution.py:148
  (1339 shorter events, 1152.1 us)
Async XLA Ops:
  6.5 1248.1 %copy-start = (bf16[512,2048]{1,0:T(8,128)(2,1)S(1)}, bf16[512,2048]{1,0:T(8,128)(2,1)}, u32[]{:S(2)}) copy-start(bf16[512,2048]{1,0:T(8,128)(2,1)} %param.15) | copy-start | bytes 6291460
  6.5 143.2 %all-gather.3.cloned.1.call-start = ((), (), s32[]{:S(2)}) async-start(), calls=%async_computation.1 | async-start | bytes 4325376 | tf_op jit(solution)/shard_map/all_gather | solution.py:34
  7.3 300.7 %all-gather.5.cloned.1.call-start = ((), (), s32[]{:S(2)}) async-start(), calls=%async_computation.2 | async-start | bytes 4325376 | tf_op jit(solution)/shard_map/all_gather | solution.py:85
  8.0 1299.9 %reduce-scatter.2.cloned.1.call-start = ((), (), s32[]{:S(2)}) async-start(), calls=%async_computation.3 | async-start | bytes 1310720 | tf_op jit(solution)/shard_map/reduce_scatter | solution.py:148
  335.6 3.6 copy-start.15
  391.8 3.6 copy-start.15
  449.1 3.6 copy-start.15
  735.9 3.6 copy-start.15
  965.3 3.6 copy-start.15
  1022.6 3.6 copy-start.15
  1079.9 3.6 copy-start.15
  1137.3 3.6 copy-start.15
  1194.6 3.6 copy-start.15
  1228.6 18.8 %copy-start.7 = (f32[512,64]{0,1:T(8,128)S(1)}, f32[512,64]{0,1:T(8,128)}, u32[]{:S(2)}) copy-start(f32[512,64]{0,1:T(8,128)} %get-tuple-element.671) | copy-start | bytes 393220
  1228.6 18.8 %copy-start.8 = (f32[512,64]{0,1:T(8,128)S(1)}, f32[512,64]{0,1:T(8,128)}, u32[]{:S(2)}) copy-start(f32[512,64]{0,1:T(8,128)} %get-tuple-element.672) | copy-start | bytes 393220
  1228.6 18.8 %copy-start.10 = (pred[64,64]{1,0:T(8,128)(4,1)S(1)}, pred[64,64]{1,0:T(8,128)(4,1)}, u32[]{:S(2)}) copy-start(pred[64,64]{1,0:T(8,128)(4,1)} %get-tuple-element.675) | copy-start | bytes 12292
  1228.6 18.7 %copy-start.11 = (pred[64,64]{1,0:T(8,128)(4,1)S(1)}, pred[64,64]{1,0:T(8,128)(4,1)}, u32[]{:S(2)}) copy-start(pred[64,64]{1,0:T(8,128)(4,1)} %get-tuple-element.676) | copy-start | bytes 12292
  1247.4 6.1 copy-start.4
  1247.4 6.1 copy-start.5
  1247.4 6.1 copy-start.9
  1247.4 6.1 copy-start.12
  1247.4 6.1 copy-start.14
  1247.5 6.6 copy-start.3
  1247.5 6.6 copy-start.13
  (55 other events, 116.5 us)
Sparse Core Ops, SparseCore 0:
  9.0 140.6 all-gather.2
  151.3 156.5 all-gather.4
  1256.2 51.6 reduce-scatter.1
where the time goes:
time: 1330 us; the launch traced here: 1320 us
  local copies, waits for them, and re-layouts  666 us (50%)
  waiting for transfers between devices  339 us (25%)
  matrix products  204 us (15%)
  other arithmetic  77.2 us (6%)
  loops' own time  15.1 us (1%)
  between operations  14.7 us (1%)
    gather x768, local copies, waits for them, and re-layouts  556 us
    all_gather x1, waiting for transfers between devices, body(): arrived = lax.all_gather(signal, 'ctx', axis=0, tiled=True)  158 us
    all_gather x1, waiting for transfers between devices, body(): whole_filter = lax.all_gather(filt, 'ctx', axis=0, tiled=True)  127 us
    dot_general x64, matrix products, transform_many(): jnp.einsum('ol,wld->wod', divide_pair_table[1], input_values, preferred_e...  114 us
    dot_general x64, matrix products, transform_many(): jnp.einsum('ol,wld->wod', divide_pair_table[0], input_values, preferred_e...  84.9 us
    reduce_scatter x1, waiting for transfers between devices, body(): lax.psum_scatter(partial_value, 'tp', scatter_dimension=1, tiled=True)  51.8 us
    add x16, other arithmetic, absorb_group(): running[3] + part_im[1]  35.1 us
  transfers between devices with their start and end apart: 3, of which 3 were waited for; matrix products, arithmetic and copies ran while one was open for 1% of the time, Pallas kernels for 0%

commit v1 on v0

--- a/solution.py
+++ b/solution.py
@@ -82,7 +82,9 @@
 
     zero_spec = jnp.zeros((frame_len, channels), jnp.float32)
     totals = (zero_spec, zero_spec, zero_spec, zero_spec)
-    arrived = lax.all_gather(signal, "ctx", axis=0, tiled=True)
+    arrived = jnp.concatenate(
+        lax.all_to_all(jnp.stack([signal] * lax.axis_size("ctx")), "ctx", 0, 0), axis=0
+    )
     block_count = arrived.shape[0] // block_len
     group = group_size()
     steps = block_count // group

time: 1330 us -> 1110 us (0.83)
  waiting for transfers between devices: 339 us -> 212 us
  matrix products: 204 us -> 143 us
  local copies, waits for them, and re-layouts: 666 us -> 627 us
    all_gather x1 -> x0, waiting for transfers between devices: 158 us -> none  [body(): arrived = lax.all_gather(signal, 'ctx', axis=0, tiled=True)]
    all_to_all x0 -> x1, waiting for transfers between devices: none -> 59 us  [body(): lax.all_to_all(jnp.stack([signal] * lax.axis_size('ctx')), 'ctx', 0, 0)]
    dot_general x64, matrix products: 114 us -> 79 us  [transform_many(): jnp.einsum('ol,wld->wod', divide_pair_table[1], input_values, preferred_e...]
    dot_general x64, matrix products: 84.9 us -> 59.1 us  [transform_many(): jnp.einsum('ol,wld->wod', divide_pair_table[0], input_values, preferred_e...]
    all_gather x1, waiting for transfers between devices: 127 us -> 104 us  [body(): whole_filter = lax.all_gather(filt, 'ctx', axis=0, tiled=True)]
    while x128 -> x416, local copies, waits for them, and re-layouts: 3.9 us -> 20.1 us
    gather x768, local copies, waits for them, and re-layouts: 556 us -> 541 us
where the time goes in v1:
time: 1110 us; the launch traced here: 1090 us
  local copies, waits for them, and re-layouts  627 us (56%)
  waiting for transfers between devices  212 us (19%)
  matrix products  143 us (13%)
  other arithmetic  70.3 us (6%)
  loops' own time  16.8 us (2%)
  between operations  14.9 us (1%)
    gather x768, local copies, waits for them, and re-layouts  541 us
    all_gather x1, waiting for transfers between devices, body(): whole_filter = lax.all_gather(filt, 'ctx', axis=0, tiled=True)  104 us
    dot_general x64, matrix products, transform_many(): jnp.einsum('ol,wld->wod', divide_pair_table[1], input_values, preferred_e...  79 us
    dot_general x64, matrix products, transform_many(): jnp.einsum('ol,wld->wod', divide_pair_table[0], input_values, preferred_e...  59.1 us
    all_to_all x1, waiting for transfers between devices, body(): lax.all_to_all(jnp.stack([signal] * lax.axis_size('ctx')), 'ctx', 0, 0)  59 us
    reduce_scatter x1, waiting for transfers between devices, body(): lax.psum_scatter(partial_value, 'tp', scatter_dimension=1, tiled=True)  48.4 us
    add x16, other arithmetic, absorb_group(): running[3] + part_im[1]  34.4 us
  transfers between devices with their start and end apart: 3, of which 3 were waited for; matrix products, arithmetic and copies ran while one was open for 1% of the time, Pallas kernels for 0%

profile of v1, /device:TPU:1, one launch (start us, length us, event | category | flops | bytes accessed | tf_op | source)
XLA Modules:
  0.0 1094.8 jit_solution(9339278396753289499)
XLA Ops:
  30.3 59.0 %all-to-all-done = bf16[32,128,512]{2,1,0:T(8,128)(2,1)} async-done(((bf16[32,128,512]{2,1,0:T(8,128)(2,1)}), bf16[32,128,512]{2,1,0:T(8,128)(2,1)}, u32[]{:S(2)}, u32[]{:S(2)}) %all-to-all-start) | async-done | bytes 4194336 | tf_op jit(solution)/shard_map/all_to_all | solution.py:86
  89.3 104.0 %all-gather.2.cloned.1.call-done = bf16[4096,512]{1,0:T(8,128)(2,1)} async-done(((bf16[128,512]{1,0:T(8,128)(2,1)}), bf16[4096,512]{1,0:T(8,128)(2,1)}) %all-gather.2.cloned.1.call-update) | async-done | bytes 4194320 | tf_op jit(solution)/shard_map/all_gather | solution.py:34
  193.3 813.5 %while.29 = (s32[]{:T(128)}, f32[128,512]{0,1:T(8,128)}, f32[128,512]{0,1:T(8,128)}, f32[128,512]{0,1:T(8,128)}, f32[128,512]{0,1:T(8,128)}, /*index=5*/s32[]{:T...) while((s32[]{:T(128)}, f32[128,512]{0,1:T(8,128)}, ...), condition=%wide.region_3.4_spmd.clone, body=%wide.region_0.3_spmd.clone.sunk | while | flops 810812544 | bytes 48664040 | solution.py:125
  218.4 17.7 %while.30 = (s32[]{:T(128)}, bf16[4096,512]{1,0:T(8,128)(2,1)}, s32[8,2]{0,1:T(2,128)S(1)}, bf16[8,127,512]{2,1,0:T(8,128)(2,1)S(1)}, s32[]{:T(128)}) while((s32[]{:T(128)}, bf16[4096,512]{1,0:T(8,128)(2,1)}, s32[8,2]{0,1:T(2,128)S(1)}, bf16[8,127,512]{2,1,0:T(8,128)(2,1)S(1)}, s32[]{:T(128)}) %tuple.94), condition=%wide.while_cond, body=%wide.while_body.sunk | while | flops 2 | bytes 261217 | solution.py:57
  268.1 17.7 %while.30 = (s32[]{:T(128)}, bf16[4096,512]{1,0:T(8,128)(2,1)}, s32[8,2]{0,1:T(2,128)S(1)}, bf16[8,127,512]{2,1,0:T(8,128)(2,1)S(1)}, s32[]{:T(128)}) while((s32[]{:T(128)}, bf16[4096,512]{1,0:T(8,128)(2,1)}, s32[8,2]{0,1:T(2,128)S(1)}, bf16[8,127,512]{2,1,0:T(8,128)(2,1)S(1)}, s32[]{:T(128)}) %tuple.94), condition=%wide.while_cond, body=%wide.while_body.sunk | while | flops 2 | bytes 261217 | solution.py:57
  319.0 17.7 %while.30 = (s32[]{:T(128)}, bf16[4096,512]{1,0:T(8,128)(2,1)}, s32[8,2]{0,1:T(2,128)S(1)}, bf16[8,127,512]{2,1,0:T(8,128)(2,1)S(1)}, s32[]{:T(128)}) while((s32[]{:T(128)}, bf16[4096,512]{1,0:T(8,128)(2,1)}, s32[8,2]{0,1:T(2,128)S(1)}, bf16[8,127,512]{2,1,0:T(8,128)(2,1)S(1)}, s32[]{:T(128)}) %tuple.94), condition=%wide.while_cond, body=%wide.while_body.sunk | while | flops 2 | bytes 261217 | solution.py:57
  369.9 17.7 %while.30 = (s32[]{:T(128)}, bf16[4096,512]{1,0:T(8,128)(2,1)}, s32[8,2]{0,1:T(2,128)S(1)}, bf16[8,127,512]{2,1,0:T(8,128)(2,1)S(1)}, s32[]{:T(128)}) while((s32[]{:T(128)}, bf16[4096,512]{1,0:T(8,128)(2,1)}, s32[8,2]{0,1:T(2,128)S(1)}, bf16[8,127,512]{2,1,0:T(8,128)(2,1)S(1)}, s32[]{:T(128)}) %tuple.94), condition=%wide.while_cond, body=%wide.while_body.sunk | while | flops 2 | bytes 261217 | solution.py:57
  420.9 17.7 %while.30 = (s32[]{:T(128)}, bf16[4096,512]{1,0:T(8,128)(2,1)}, s32[8,2]{0,1:T(2,128)S(1)}, bf16[8,127,512]{2,1,0:T(8,128)(2,1)S(1)}, s32[]{:T(128)}) while((s32[]{:T(128)}, bf16[4096,512]{1,0:T(8,128)(2,1)}, s32[8,2]{0,1:T(2,128)S(1)}, bf16[8,127,512]{2,1,0:T(8,128)(2,1)S(1)}, s32[]{:T(128)}) %tuple.94), condition=%wide.while_cond, body=%wide.while_body.sunk | while | flops 2 | bytes 261217 | solution.py:57
  449.5 16.3 %while.31 = (s32[]{:T(128)}, s32[4096]{0:T(1024)}, s32[8,1]{0,1:T(1,128)S(1)}, s32[8,64]{1,0:T(8,128)S(1)}, s32[]{:T(128)}, /*index=5*/s32[]{:T(128)}) while((s32[]{:T(128)}, s32[4096]{0:T(1024)}, s32[8,1]{0,1:T(1,128)S(1)}, s32[8,64]{1,0:T(8,128)S(1)}, s32[]{:T(128)}, /*index=5*/s32[]{:T(128)}) %tuple.97), condition=%wide.while_cond.1, body=%wide.while_body.1.sunk | while | flops 2 | bytes 1113 | solution.py:54
  471.8 17.7 %while.30 = (s32[]{:T(128)}, bf16[4096,512]{1,0:T(8,128)(2,1)}, s32[8,2]{0,1:T(2,128)S(1)}, bf16[8,127,512]{2,1,0:T(8,128)(2,1)S(1)}, s32[]{:T(128)}) while((s32[]{:T(128)}, bf16[4096,512]{1,0:T(8,128)(2,1)}, s32[8,2]{0,1:T(2,128)S(1)}, bf16[8,127,512]{2,1,0:T(8,128)(2,1)S(1)}, s32[]{:T(128)}) %tuple.94), condition=%wide.while_cond, body=%wide.while_body.sunk | while | flops 2 | bytes 261217 | solution.py:57
  500.5 16.3 %while.31 = (s32[]{:T(128)}, s32[4096]{0:T(1024)}, s32[8,1]{0,1:T(1,128)S(1)}, s32[8,64]{1,0:T(8,128)S(1)}, s32[]{:T(128)}, /*index=5*/s32[]{:T(128)}) while((s32[]{:T(128)}, s32[4096]{0:T(1024)}, s32[8,1]{0,1:T(1,128)S(1)}, s32[8,64]{1,0:T(8,128)S(1)}, s32[]{:T(128)}, /*index=5*/s32[]{:T(128)}) %tuple.97), condition=%wide.while_cond.1, body=%wide.while_body.1.sunk | while | flops 2 | bytes 1113 | solution.py:54
  522.7 17.7 %while.30 = (s32[]{:T(128)}, bf16[4096,512]{1,0:T(8,128)(2,1)}, s32[8,2]{0,1:T(2,128)S(1)}, bf16[8,127,512]{2,1,0:T(8,128)(2,1)S(1)}, s32[]{:T(128)}) while((s32[]{:T(128)}, bf16[4096,512]{1,0:T(8,128)(2,1)}, s32[8,2]{0,1:T(2,128)S(1)}, bf16[8,127,512]{2,1,0:T(8,128)(2,1)S(1)}, s32[]{:T(128)}) %tuple.94), condition=%wide.while_cond, body=%wide.while_body.sunk | while | flops 2 | bytes 261217 | solution.py:57
  573.7 17.7 %while.30 = (s32[]{:T(128)}, bf16[4096,512]{1,0:T(8,128)(2,1)}, s32[8,2]{0,1:T(2,128)S(1)}, bf16[8,127,512]{2,1,0:T(8,128)(2,1)S(1)}, s32[]{:T(128)}) while((s32[]{:T(128)}, bf16[4096,512]{1,0:T(8,128)(2,1)}, s32[8,2]{0,1:T(2,128)S(1)}, bf16[8,127,512]{2,1,0:T(8,128)(2,1)S(1)}, s32[]{:T(128)}) %tuple.94), condition=%wide.while_cond, body=%wide.while_body.sunk | while | flops 2 | bytes 261217 | solution.py:57
  624.6 17.7 %while.30 = (s32[]{:T(128)}, bf16[4096,512]{1,0:T(8,128)(2,1)}, s32[8,2]{0,1:T(2,128)S(1)}, bf16[8,127,512]{2,1,0:T(8,128)(2,1)S(1)}, s32[]{:T(128)}) while((s32[]{:T(128)}, bf16[4096,512]{1,0:T(8,128)(2,1)}, s32[8,2]{0,1:T(2,128)S(1)}, bf16[8,127,512]{2,1,0:T(8,128)(2,1)S(1)}, s32[]{:T(128)}) %tuple.94), condition=%wide.while_cond, body=%wide.while_body.sunk | while | flops 2 | bytes 261217 | solution.py:57
  653.2 16.3 %while.31 = (s32[]{:T(128)}, s32[4096]{0:T(1024)}, s32[8,1]{0,1:T(1,128)S(1)}, s32[8,64]{1,0:T(8,128)S(1)}, s32[]{:T(128)}, /*index=5*/s32[]{:T(128)}) while((s32[]{:T(128)}, s32[4096]{0:T(1024)}, s32[8,1]{0,1:T(1,128)S(1)}, s32[8,64]{1,0:T(8,128)S(1)}, s32[]{:T(128)}, /*index=5*/s32[]{:T(128)}) %tuple.97), condition=%wide.while_cond.1, body=%wide.while_body.1.sunk | while | flops 2 | bytes 1113 | solution.py:54
  675.5 17.7 %while.30 = (s32[]{:T(128)}, bf16[4096,512]{1,0:T(8,128)(2,1)}, s32[8,2]{0,1:T(2,128)S(1)}, bf16[8,127,512]{2,1,0:T(8,128)(2,1)S(1)}, s32[]{:T(128)}) while((s32[]{:T(128)}, bf16[4096,512]{1,0:T(8,128)(2,1)}, s32[8,2]{0,1:T(2,128)S(1)}, bf16[8,127,512]{2,1,0:T(8,128)(2,1)S(1)}, s32[]{:T(128)}) %tuple.94), condition=%wide.while_cond, body=%wide.while_body.sunk | while | flops 2 | bytes 261217 | solution.py:57
  726.4 17.7 %while.30 = (s32[]{:T(128)}, bf16[4096,512]{1,0:T(8,128)(2,1)}, s32[8,2]{0,1:T(2,128)S(1)}, bf16[8,127,512]{2,1,0:T(8,128)(2,1)S(1)}, s32[]{:T(128)}) while((s32[]{:T(128)}, bf16[4096,512]{1,0:T(8,128)(2,1)}, s32[8,2]{0,1:T(2,128)S(1)}, bf16[8,127,512]{2,1,0:T(8,128)(2,1)S(1)}, s32[]{:T(128)}) %tuple.94), condition=%wide.while_cond, body=%wide.while_body.sunk | while | flops 2 | bytes 261217 | solution.py:57
  777.3 17.7 %while.30 = (s32[]{:T(128)}, bf16[4096,512]{1,0:T(8,128)(2,1)}, s32[8,2]{0,1:T(2,128)S(1)}, bf16[8,127,512]{2,1,0:T(8,128)(2,1)S(1)}, s32[]{:T(128)}) while((s32[]{:T(128)}, bf16[4096,512]{1,0:T(8,128)(2,1)}, s32[8,2]{0,1:T(2,128)S(1)}, bf16[8,127,512]{2,1,0:T(8,128)(2,1)S(1)}, s32[]{:T(128)}) %tuple.94), condition=%wide.while_cond, body=%wide.while_body.sunk | while | flops 2 | bytes 261217 | solution.py:57
  828.2 17.7 %while.30 = (s32[]{:T(128)}, bf16[4096,512]{1,0:T(8,128)(2,1)}, s32[8,2]{0,1:T(2,128)S(1)}, bf16[8,127,512]{2,1,0:T(8,128)(2,1)S(1)}, s32[]{:T(128)}) while((s32[]{:T(128)}, bf16[4096,512]{1,0:T(8,128)(2,1)}, s32[8,2]{0,1:T(2,128)S(1)}, bf16[8,127,512]{2,1,0:T(8,128)(2,1)S(1)}, s32[]{:T(128)}) %tuple.94), condition=%wide.while_cond, body=%wide.while_body.sunk | while | flops 2 | bytes 261217 | solution.py:57
  879.2 17.7 %while.30 = (s32[]{:T(128)}, bf16[4096,512]{1,0:T(8,128)(2,1)}, s32[8,2]{0,1:T(2,128)S(1)}, bf16[8,127,512]{2,1,0:T(8,128)(2,1)S(1)}, s32[]{:T(128)}) while((s32[]{:T(128)}, bf16[4096,512]{1,0:T(8,128)(2,1)}, s32[8,2]{0,1:T(2,128)S(1)}, bf16[8,127,512]{2,1,0:T(8,128)(2,1)S(1)}, s32[]{:T(128)}) %tuple.94), condition=%wide.while_cond, body=%wide.while_body.sunk | while | flops 2 | bytes 261217 | solution.py:57
  930.1 17.7 %while.30 = (s32[]{:T(128)}, bf16[4096,512]{1,0:T(8,128)(2,1)}, s32[8,2]{0,1:T(2,128)S(1)}, bf16[8,127,512]{2,1,0:T(8,128)(2,1)S(1)}, s32[]{:T(128)}) while((s32[]{:T(128)}, bf16[4096,512]{1,0:T(8,128)(2,1)}, s32[8,2]{0,1:T(2,128)S(1)}, bf16[8,127,512]{2,1,0:T(8,128)(2,1)S(1)}, s32[]{:T(128)}) %tuple.94), condition=%wide.while_cond, body=%wide.while_body.sunk | while | flops 2 | bytes 261217 | solution.py:57
  981.0 17.7 %while.30 = (s32[]{:T(128)}, bf16[4096,512]{1,0:T(8,128)(2,1)}, s32[8,2]{0,1:T(2,128)S(1)}, bf16[8,127,512]{2,1,0:T(8,128)(2,1)S(1)}, s32[]{:T(128)}) while((s32[]{:T(128)}, bf16[4096,512]{1,0:T(8,128)(2,1)}, s32[8,2]{0,1:T(2,128)S(1)}, bf16[8,127,512]{2,1,0:T(8,128)(2,1)S(1)}, s32[]{:T(128)}) %tuple.94), condition=%wide.while_cond, body=%wide.while_body.sunk | while | flops 2 | bytes 261217 | solution.py:57
  1010.6 18.7 %gather_fusion = bf16[4096,512]{1,0:T(8,128)(2,1)} fusion(bf16[64,512]{1,0:T(8,128)(2,1)S(1)} %slice.146, s32[4096]{0:T(1024)} %broadcast_clamp_fusion), kind=kCustom, calls=%fused_computation | custom fusion | bytes 8404992 | tf_op jit(solution)/shard_map/gather | solution.py:134
  1037.9 48.4 %reduce-scatter.2.cloned.1.call-done = f32[128,512]{1,0:T(8,128)} async-done(((f32[128,2048]{1,0:T(8,128)}), f32[128,512]{1,0:T(8,128)}) %reduce-scatter.2.cloned.1.call-update) | async-done | bytes 262160 | tf_op jit(solution)/shard_map/reduce_scatter | solution.py:150
  (1629 shorter events, 1045.1 us)
Async XLA Ops:
  6.5 1030.0 %copy-start = (bf16[512,2048]{1,0:T(8,128)(2,1)S(1)}, bf16[512,2048]{1,0:T(8,128)(2,1)}, u32[]{:S(2)}) copy-start(bf16[512,2048]{1,0:T(8,128)(2,1)} %param.15) | copy-start | bytes 6291460
  6.5 186.8 %all-gather.2.cloned.1.call-start = ((), (), s32[]{:S(2)}) async-start(), calls=%async_computation.2 | async-start | bytes 4325376 | tf_op jit(solution)/shard_map/all_gather | solution.py:34
  10.6 78.7 %all-to-all-start = ((bf16[32,128,512]{2,1,0:T(8,128)(2,1)}), bf16[32,128,512]{2,1,0:T(8,128)(2,1)}, u32[]{:S(2)}, u32[]{:S(2)}) async-start(bf16[32,128,512]{2,1,0:T(8,128)(2,1)} %stack.2), calls=%async_computation | async-start | bytes 8388608 | tf_op jit(solution)/shard_map/all_to_all | solution.py:86
  20.6 1065.8 %reduce-scatter.2.cloned.1.call-start = ((), (), s32[]{:S(2)}) async-start(), calls=%async_computation.3 | async-start | bytes 1310720 | tf_op jit(solution)/shard_map/reduce_scatter | solution.py:150
  193.3 19.3 %copy-start.17 = (s32[]{:T(128)}, s32[]{:T(128)S(1)}, u32[]{:S(2)}) copy-start(s32[]{:T(128)S(1)} %get-tuple-element.1003) | copy-start | bytes 16 | tf_op jit(solution)/shard_map/while
  243.1 19.3 %copy-start.17 = (s32[]{:T(128)}, s32[]{:T(128)S(1)}, u32[]{:S(2)}) copy-start(s32[]{:T(128)S(1)} %get-tuple-element.1003) | copy-start | bytes 16 | tf_op jit(solution)/shard_map/while
  294.0 19.3 %copy-start.17 = (s32[]{:T(128)}, s32[]{:T(128)S(1)}, u32[]{:S(2)}) copy-start(s32[]{:T(128)S(1)} %get-tuple-element.1003) | copy-start | bytes 16 | tf_op jit(solution)/shard_map/while
  344.9 19.3 %copy-start.17 = (s32[]{:T(128)}, s32[]{:T(128)S(1)}, u32[]{:S(2)}) copy-start(s32[]{:T(128)S(1)} %get-tuple-element.1003) | copy-start | bytes 16 | tf_op jit(solution)/shard_map/while
  395.8 19.3 %copy-start.17 = (s32[]{:T(128)}, s32[]{:T(128)S(1)}, u32[]{:S(2)}) copy-start(s32[]{:T(128)S(1)} %get-tuple-element.1003) | copy-start | bytes 16 | tf_op jit(solution)/shard_map/while
  446.7 19.2 %copy-start.15 = (s32[]{:T(128)}, s32[]{:T(128)S(1)}, u32[]{:S(2)}) copy-start(s32[]{:T(128)S(1)} %get-tuple-element.1004) | copy-start | bytes 16 | tf_op jit(solution)/shard_map/while
  446.7 19.3 %copy-start.17 = (s32[]{:T(128)}, s32[]{:T(128)S(1)}, u32[]{:S(2)}) copy-start(s32[]{:T(128)S(1)} %get-tuple-element.1003) | copy-start | bytes 16 | tf_op jit(solution)/shard_map/while
  497.6 19.2 %copy-start.15 = (s32[]{:T(128)}, s32[]{:T(128)S(1)}, u32[]{:S(2)}) copy-start(s32[]{:T(128)S(1)} %get-tuple-element.1004) | copy-start | bytes 16 | tf_op jit(solution)/shard_map/while
  497.6 19.3 %copy-start.17 = (s32[]{:T(128)}, s32[]{:T(128)S(1)}, u32[]{:S(2)}) copy-start(s32[]{:T(128)S(1)} %get-tuple-element.1003) | copy-start | bytes 16 | tf_op jit(solution)/shard_map/while
  548.6 19.2 %copy-start.15 = (s32[]{:T(128)}, s32[]{:T(128)S(1)}, u32[]{:S(2)}) copy-start(s32[]{:T(128)S(1)} %get-tuple-element.1004) | copy-start | bytes 16 | tf_op jit(solution)/shard_map/while
  548.6 19.3 %copy-start.17 = (s32[]{:T(128)}, s32[]{:T(128)S(1)}, u32[]{:S(2)}) copy-start(s32[]{:T(128)S(1)} %get-tuple-element.1003) | copy-start | bytes 16 | tf_op jit(solution)/shard_map/while
  599.5 19.3 %copy-start.17 = (s32[]{:T(128)}, s32[]{:T(128)S(1)}, u32[]{:S(2)}) copy-start(s32[]{:T(128)S(1)} %get-tuple-element.1003) | copy-start | bytes 16 | tf_op jit(solution)/shard_map/while
  650.4 19.3 %copy-start.17 = (s32[]{:T(128)}, s32[]{:T(128)S(1)}, u32[]{:S(2)}) copy-start(s32[]{:T(128)S(1)} %get-tuple-element.1003) | copy-start | bytes 16 | tf_op jit(solution)/shard_map/while
  701.4 19.2 %copy-start.15 = (s32[]{:T(128)}, s32[]{:T(128)S(1)}, u32[]{:S(2)}) copy-start(s32[]{:T(128)S(1)} %get-tuple-element.1004) | copy-start | bytes 16 | tf_op jit(solution)/shard_map/while
  701.4 19.3 %copy-start.17 = (s32[]{:T(128)}, s32[]{:T(128)S(1)}, u32[]{:S(2)}) copy-start(s32[]{:T(128)S(1)} %get-tuple-element.1003) | copy-start | bytes 16 | tf_op jit(solution)/shard_map/while
  752.3 19.3 %copy-start.17 = (s32[]{:T(128)}, s32[]{:T(128)S(1)}, u32[]{:S(2)}) copy-start(s32[]{:T(128)S(1)} %get-tuple-element.1003) | copy-start | bytes 16 | tf_op jit(solution)/shard_map/while
  803.2 19.3 %copy-start.17 = (s32[]{:T(128)}, s32[]{:T(128)S(1)}, u32[]{:S(2)}) copy-start(s32[]{:T(128)S(1)} %get-tuple-element.1003) | copy-start | bytes 16 | tf_op jit(solution)/shard_map/while
  854.1 19.3 %copy-start.17 = (s32[]{:T(128)}, s32[]{:T(128)S(1)}, u32[]{:S(2)}) copy-start(s32[]{:T(128)S(1)} %get-tuple-element.1003) | copy-start | bytes 16 | tf_op jit(solution)/shard_map/while
  905.0 19.3 %copy-start.17 = (s32[]{:T(128)}, s32[]{:T(128)S(1)}, u32[]{:S(2)}) copy-start(s32[]{:T(128)S(1)} %get-tuple-element.1003) | copy-start | bytes 16 | tf_op jit(solution)/shard_map/while
  955.9 19.3 %copy-start.17 = (s32[]{:T(128)}, s32[]{:T(128)S(1)}, u32[]{:S(2)}) copy-start(s32[]{:T(128)S(1)} %get-tuple-element.1003) | copy-start | bytes 16 | tf_op jit(solution)/shard_map/while
  (200 other events, 650.9 us)
Sparse Core Ops, SparseCore 0:
  9.0 184.2 all-gather.1
  1038.1 48.2 reduce-scatter.1
